TPU v7x, 32 devices: a whole 2x2x4 slice. The times are simulated.
32 devices in a mesh: req: 8 (over z, y), tp: 4 (over x, core).
Axes of the slice: x: 2, y: 2, z: 4, core: 2. Of those that a mesh axis runs over, the one named last changes fastest.
Arguments:
- tokens: bfloat16 [16, 1024], P('req'), may hold values from -4 to 4
- slot_of: int32 [16], replicated, may hold values from 0 to 15, each once
- key_cache: bfloat16 [16, 1536, 1024], P('req', None, 'tp'), may hold values from -1100 to 1100
- value_cache: bfloat16 [16, 1536, 1024], P('req', None, 'tp'), may hold values from -6 to 6
- cache_len: int32 [16], P('req'), may hold values from 1 to 1536, as said below
- rel_bucket: int32 [16, 1536], P('req'), may hold values from 0 to 511
- rel_table: bfloat16 [512, 1024], P('req'), may hold values from -6 to 6
- w_query: bfloat16 [1024, 1024], P(None, 'tp'), may hold values from -0.1875 to 0.1875
- w_key: bfloat16 [1024, 1024], P(None, 'tp'), may hold values from -0.1875 to 0.1875
- w_out: bfloat16 [1024, 1024], P('tp'), may hold values from -0.1875 to 0.1875
- out_gain: float32 [1024], P('tp'), may hold values from 0.1 to 1.9
- out_bias: float32 [1024], P('tp'), may hold values from -0.5 to 0.5
Outputs:
- normed: bfloat16 [16, 1024], P('req', 'tp')
Inputs may be any that keep to these rules, and one draw needn't show every extreme that they name: slot_of names every slot exactly once. `cache_len`: some slot holds exactly 1536 live positions in every draw.
All inputs are finite; a program needn't handle non-finite values.
Results may differ from a plain program's by a relative error of at most 0.0034.
The roundings to bfloat16 on the way count: a program that leaves them out, or rounds other values in their place, can miss the bound.
Values may be sent and summed in bfloat16 or wider, within the bound.
No kernel may reach another device: no remote copies, remote signals or barrier semaphores. Data moves between devices by JAX's collectives and lax.ppermute only.
A program may use at most 64 MiB of HBM per device.

v0:
```python
import math
import jax
import jax.numpy as jnp
from jax import lax
from jax.sharding import PartitionSpec as P

HD = 64
BUCKETS = 512
MAXLEN = 1536
BLOCK = 512
epsilon = 1e-06
masked_score = -1e30


def norm_rows(matrix):
    row_mean = jnp.mean(matrix, axis=-1, keepdims=True)
    centred = matrix - row_mean
    variance = jnp.mean(centred * centred, axis=-1, keepdims=True)
    return centred * lax.rsqrt(variance + epsilon)


def project_rows(shard_rows, w_key, w_query):
    normed_rows = norm_rows(shard_rows.astype(jnp.float32)).astype(jnp.bfloat16)
    key_part = jnp.dot(normed_rows, w_key, preferred_element_type=jnp.float32).astype(jnp.bfloat16)
    query_part = jnp.dot(normed_rows, w_query, preferred_element_type=jnp.float32).astype(
        jnp.bfloat16
    )
    return jnp.concatenate((key_part, query_part), axis=1)


def block_scores(offset, key_rows, bucket_rows, query_heads, rel_key, rel_query):
    local_heads = query_heads.shape[0]
    block_keys = lax.dynamic_slice_in_dim(key_rows, offset, BLOCK, 0)
    forward = lax.dynamic_slice_in_dim(bucket_rows, offset, BLOCK, 0)
    backward = jnp.minimum(BUCKETS - forward, BUCKETS - 1)
    table_ids = jnp.arange(BUCKETS, dtype=jnp.int32)
    one_fwd = (forward[:, None] == table_ids[None, :]).astype(jnp.bfloat16)
    one_back = (backward[:, None] == table_ids[None, :]).astype(jnp.bfloat16)
    rows_fwd = jnp.dot(one_fwd, rel_key, preferred_element_type=jnp.float32).reshape(
        BLOCK, local_heads, HD
    )
    rows_back = jnp.dot(one_back, rel_query, preferred_element_type=jnp.float32).reshape(
        BLOCK, local_heads, HD
    )
    key_heads = block_keys.reshape(BLOCK, local_heads, HD)
    content = jnp.einsum("hd,jhd->hj", query_heads, key_heads, preferred_element_type=jnp.float32)
    along_key = jnp.einsum("hd,jhd->hj", query_heads.astype(jnp.float32), rows_fwd)
    against = jnp.sum(key_heads.astype(jnp.float32) * rows_back, axis=2).T
    return (content + along_key + against) * (1.0 / math.sqrt(3.0 * HD))


def attend_slot(query_own, key_rows, value_rows, bucket_rows, length, rel_key, rel_query):
    local_heads = query_own.shape[0] // HD
    query_heads = query_own.reshape(local_heads, HD)
    block_count = (length + BLOCK - 1) // BLOCK

    def block_step(block_index, buffer):
        offset = block_index * BLOCK
        block_part = block_scores(offset, key_rows, bucket_rows, query_heads, rel_key, rel_query)
        return lax.dynamic_update_slice_in_dim(buffer, block_part, offset, 1)

    scores = lax.fori_loop(
        0, block_count, block_step, jnp.full((local_heads, MAXLEN), masked_score, jnp.float32)
    )
    positions = jnp.arange(MAXLEN, dtype=jnp.int32)
    live_keys = (positions < length)[None, :]
    scores = jnp.where(live_keys, scores, masked_score)
    highest = jnp.max(scores, axis=1, keepdims=True)
    exponent = jnp.where(live_keys, jnp.exp(scores - highest), 0.0)
    weights = (exponent / jnp.sum(exponent, axis=1, keepdims=True)).astype(jnp.bfloat16)
    value_heads = value_rows.reshape(MAXLEN, local_heads, HD)
    context = jnp.einsum("hj,jhd->hd", weights, value_heads, preferred_element_type=jnp.float32)
    return context.reshape(local_heads * HD).astype(jnp.bfloat16)


def per_device(
    tokens,
    slot_of,
    key_cache,
    value_cache,
    cache_len,
    rel_bucket,
    rel_table,
    w_query,
    w_key,
    w_out,
    out_gain,
    out_bias,
):
    rows_dev = tokens.shape[0]
    col_width = w_query.shape[1]
    rel_both = project_rows(lax.all_gather(rel_table, "req", axis=0, tiled=True), w_key, w_query)
    rel_key = rel_both[:, :col_width]
    rel_query = rel_both[:, col_width:]
    queries = jnp.dot(tokens, w_query, preferred_element_type=jnp.float32).astype(jnp.bfloat16)
    all_queries = lax.all_gather(queries, "req", axis=0, tiled=True)
    first_row = lax.axis_index("req") * rows_dev
    own_rows = first_row + jnp.arange(rows_dev, dtype=jnp.int32)
    request_count = slot_of.shape[0]
    chooser = (slot_of[None, :] == own_rows[:, None]).astype(jnp.bfloat16)
    own_queries = jnp.dot(chooser, all_queries, preferred_element_type=jnp.float32).astype(
        jnp.bfloat16
    )
    contexts = []
    for slot_index in range(rows_dev):
        contexts.append(
            attend_slot(
                own_queries[slot_index],
                key_cache[slot_index],
                value_cache[slot_index],
                rel_bucket[slot_index],
                cache_len[slot_index],
                rel_key,
                rel_query,
            )
        )
    own_context = jnp.stack(contexts, axis=0)
    all_contexts = lax.all_gather(own_context, "req", axis=0, tiled=True)
    own_slots = lax.dynamic_slice_in_dim(slot_of, first_row, rows_dev, 0)
    picker = (own_slots[:, None] == jnp.arange(request_count, dtype=jnp.int32)[None, :]).astype(
        jnp.bfloat16
    )
    context_rows = jnp.dot(picker, all_contexts, preferred_element_type=jnp.float32).astype(
        jnp.bfloat16
    )
    partial_out = jnp.dot(context_rows, w_out, preferred_element_type=jnp.float32)
    col_start = lax.axis_index("tp") * col_width
    row_sum = lax.psum(partial_out, "tp")
    normed_full = norm_rows(row_sum + tokens.astype(jnp.float32))
    own_cols = lax.dynamic_slice_in_dim(normed_full, col_start, col_width, 1)
    return (own_cols * out_gain + out_bias).astype(jnp.bfloat16)


def solution(mesh):
    in_specs = (
        P("req", None),
        P(),
        P("req", None, "tp"),
        P("req", None, "tp"),
        P("req"),
        P("req", None),
        P("req", None),
        P(None, "tp"),
        P(None, "tp"),
        P("tp", None),
        P("tp"),
        P("tp"),
    )
    out_specs = P("req", "tp")
    return jax.shard_map(
        per_device, mesh=mesh, in_specs=in_specs, out_specs=out_specs, check_vma=False
    )
```

profile of v0, /device:TPU:0, one launch (start us, length us, event | category | flops | bytes accessed | tf_op | source)
XLA Modules:
  0.0 98.8 jit_solution(9995086282330034420)
XLA Ops:
  6.5 0.7 all-gather.4.cloned.1.call-update
  7.3 1.4 %fusion.53 = (s32[1]{0:T(128)}, s32[1]{0:T(128)}) fusion(s32[2]{0:T(128)} %param.20), kind=kLoop, calls=%fused_computation.89 | loop fusion | bytes 16 | tf_op jit(solution)/shard_map/slice | solution.py:112
  10.1 0.9 fusion.25
  10.9 22.3 %all-gather = bf16[8,2,256]{2,1,0:T(2,128)(2,1)S(1)} all-gather(bf16[1,2,256]{2,1,0:T(2,128)(2,1)S(1)} %fusion.25), channel_id=1, replica_groups=mesh['req'=8,'tp'=4] {'req'}, dimensions={0}, use_global_device_ids=true | all-gather | bytes 9216 | tf_op jit(solution)/shard_map/all_gather | solution.py:96
  33.2 0.7 dynamic_slice.18
  33.9 0.8 convolution_convert_fusion.4
  34.8 0.1 reshape_squeeze.12
  34.9 0.1 reshape_squeeze.14
  35.0 1.5 %fusion.51 = (bf16[1,1536,256]{2,1,0:T(8,128)(2,1)S(1)}, bf16[1,1536,256]{2,1,0:T(8,128)(2,1)S(1)}) fusion(bf16[2,1536,256]{2,1,0:T(8,128)(2,1)} %param.18), kind=kLoop, calls=%fused_computation.87 | loop fusion | bytes 3145728 | tf_op jit(solution)/shard_map/slice | solution.py:109
  36.5 1.2 %copy.33 = bf16[1,1536,256]{1,2,0:T(8,128)(2,1)} copy(bf16[1,1536,256]{2,1,0:T(8,128)(2,1)S(1)} %get-tuple-element.139) | data formatting | bytes 1572864
  37.6 1.2 %copy.35 = bf16[1,1536,256]{1,2,0:T(8,128)(2,1)} copy(bf16[1,1536,256]{2,1,0:T(8,128)(2,1)S(1)} %get-tuple-element.140) | data formatting | bytes 1572864
  38.8 1.5 %fusion.52 = (bf16[1,1536,256]{2,1,0:T(8,128)(2,1)S(1)}, bf16[1,1536,256]{2,1,0:T(8,128)(2,1)S(1)}) fusion(bf16[2,1536,256]{2,1,0:T(8,128)(2,1)} %param.19), kind=kLoop, calls=%fused_computation.88 | loop fusion | bytes 3145728 | tf_op jit(solution)/shard_map/slice | solution.py:110
  40.3 0.3 copy.34
  40.6 0.3 copy.36
  40.9 0.7 iota_compare_fusion.9
  41.6 0.7 iota_compare_fusion.8
  42.3 10.1 %all-gather.4.cloned.1.call-done = bf16[512,1024]{1,0:T(8,128)(2,1)} async-done(((bf16[64,1024]{1,0:T(8,128)(2,1)}), bf16[512,1024]{1,0:T(8,128)(2,1)}) %all-gather.4.cloned.1.call-update) | async-done | bytes 1048592 | tf_op jit(solution)/shard_map/all_gather | solution.py:92
  52.5 1.5 %convert_reduce_fusion = f32[512]{0:T(512)S(1)} fusion(bf16[512,1024]{1,0:T(8,128)(2,1)} %all-gather.4.cloned.1.call-done), kind=kLoop, calls=%fused_computation.35 | loop fusion | flops 1048064 | bytes 1050624 | tf_op jit(solution)/shard_map/reduce_sum | solution.py:16
  54.0 0.4 fusion.22
  54.4 0.5 convolution_convert_fusion
  54.9 0.5 copy-done.7
  55.5 0.5 convolution_convert_fusion.1
  56.0 2.4 %while.20 = (s32[]{:T(128)}, f32[4,1536]{1,0:T(4,128)S(1)}, s32[]{:T(128)}, bf16[1536,256]{0,1:T(8,128)(2,1)}, bf16[4,64]{1,0:T(4,128)(2,1)S(1)}, /*index=5*/s32...) while((s32[]{:T(128)}, f32[4,1536]{1,0:T(4,128)S(1)}, ...), condition=%wide.region_4.5_spmd, body=%wide.region_2.4_spmd.sunk | while | flops 269882368 | bytes 1903791 | solution.py:62
  56.1 0.5 fusion.97
  56.6 0.1 fusion.98
  56.7 1.5 %multiply_reduce_fusion.5 = (f32[512,4]{0,1:T(4,128)S(1)}, bf16[512,256]{0,1:T(8,128)(2,1)S(1)}) fusion(bf16[1536,256]{0,1:T(8,128)(2,1)} %get-tuple-element.324, s32[]{:T(128)S(6)} %select_n.77, bf16[512,256]{1,0:T(8,128)(2,1)S(1)} %get-tuple-element.328, s32[512]{0:T(512)S(1)} %get-tuple-element.245), kind=kOutput, calls=%fused_computation.4.clone.1 | convolution fusion | flops 134871040 | bytes 796676 | tf_op jit(solution)/shard_map/while/body/dot_general | solution.py:42
  58.2 0.1 fusion.99
  58.4 0.1 select_reduce_fusion.1
  58.5 0.2 fusion.30
  58.7 0.1 fusion.32
  58.8 2.4 %while.21 = (s32[]{:T(128)}, f32[4,1536]{1,0:T(4,128)S(1)}, s32[]{:T(128)}, bf16[1536,256]{0,1:T(8,128)(2,1)}, bf16[4,64]{1,0:T(4,128)(2,1)S(1)}, /*index=5*/s32...) while((s32[]{:T(128)}, f32[4,1536]{1,0:T(4,128)S(1)}, ...), condition=%wide.region_9.10_spmd, body=%wide.region_7.9_spmd.sunk | while | flops 269882368 | bytes 1903791 | solution.py:62
  58.9 0.5 fusion.107
  59.4 0.1 fusion.108
  59.6 1.5 %multiply_reduce_fusion.6 = (f32[512,4]{0,1:T(4,128)S(1)}, bf16[512,256]{0,1:T(8,128)(2,1)S(1)}) fusion(bf16[1536,256]{0,1:T(8,128)(2,1)} %get-tuple-element.288, s32[]{:T(128)S(6)} %select_n.78, bf16[512,256]{1,0:T(8,128)(2,1)S(1)} %get-tuple-element.292, s32[512]{0:T(512)S(1)} %get-tuple-element.257), kind=kOutput, calls=%fused_computation.21.clone.1 | convolution fusion | flops 134871040 | bytes 796676 | tf_op jit(solution)/shard_map/while/body/dot_general | solution.py:42
  61.1 0.1 fusion.109
  61.3 0.1 select_reduce_fusion
  61.4 0.2 fusion.31
  61.6 0.1 fusion.33
  61.7 0.3 fusion.28
  62.0 0.1 convert_element_type.81
  62.1 0.3 fusion.26
  62.4 0.1 convert_element_type.84
  62.6 22.3 %all-gather.1 = bf16[8,2,256]{2,1,0:T(2,128)(2,1)S(1)} all-gather(bf16[1,2,256]{2,1,0:T(2,128)(2,1)S(1)} %maximum_bitcast_fusion), channel_id=1, replica_groups=mesh['req'=8,'tp'=4] {'req'}, dimensions={0}, use_global_device_ids=true | all-gather | bytes 9216 | tf_op jit(solution)/shard_map/all_gather | solution.py:118
  84.9 0.3 fusion.24
  85.2 5.7 %psum.7 = f32[2,1024]{1,0:T(2,128)S(1)} all-reduce(f32[2,1024]{1,0:T(2,128)S(1)} %fusion.24), channel_id=1, replica_groups=mesh['req'=8,'tp'=4] {'tp'}, use_global_device_ids=true, to_apply=%region_12.13 | all-reduce | flops 2048 | bytes 16384 | tf_op jit(solution)/shard_map/psum | solution.py:128
  91.0 0.1 fusion.35
  91.1 0.2 multiply_reduce_fusion.2
  91.3 0.6 fusion.38
  (34 shorter events, 0.4 us)
Async XLA Ops:
  6.5 3.5 %copy-start = (bf16[1024,256]{1,0:T(8,128)(2,1)S(1)}, bf16[1024,256]{1,0:T(8,128)(2,1)}, u32[]{:S(2)}) copy-start(bf16[1024,256]{1,0:T(8,128)(2,1)} %param.23) | copy-start | bytes 1572868
  6.5 45.9 %all-gather.4.cloned.1.call-start = ((), (), s32[]{:S(2)}) async-start(), calls=%async_computation | async-start | bytes 1179648 | tf_op jit(solution)/shard_map/all_gather | solution.py:92
  40.3 2.0 %copy-start.4 = (s32[2,1536]{1,0:T(2,128)S(1)}, s32[2,1536]{1,0:T(2,128)}, u32[]{:S(2)}) copy-start(s32[2,1536]{1,0:T(2,128)} %param.21) | copy-start | bytes 36868
  52.5 1.5 %copy-start.1 = (bf16[512,1024]{1,0:T(8,128)(2,1)S(1)}, bf16[512,1024]{1,0:T(8,128)(2,1)}, u32[]{:S(2)}) copy-start(bf16[512,1024]{1,0:T(8,128)(2,1)} %all-gather.4.cloned.1.call-done) | copy-start | bytes 3145732
  54.4 1.0 %copy-start.7 = (bf16[1024,256]{1,0:T(8,128)(2,1)S(1)}, bf16[1024,256]{1,0:T(8,128)(2,1)}, u32[]{:S(2)}) copy-start(bf16[1024,256]{1,0:T(8,128)(2,1)} %param.24) | copy-start | bytes 1572868
  61.2 23.7 %copy-start.2 = (bf16[256,1024]{1,0:T(8,128)(2,1)S(1)}, bf16[256,1024]{1,0:T(8,128)(2,1)}, u32[]{:S(2)}) copy-start(bf16[256,1024]{1,0:T(8,128)(2,1)} %param.25) | copy-start | bytes 1572868
  61.3 29.7 %copy-start.3 = (bf16[2,1024]{1,0:T(2,128)(2,1)S(1)}, bf16[2,1024]{1,0:T(2,128)(2,1)}, u32[]{:S(2)}) copy-start(bf16[2,1024]{1,0:T(2,128)(2,1)} %param.16) | copy-start | bytes 12292
  61.3 30.1 %copy-start.5 = (f32[256]{0:T(256)S(1)}, f32[256]{0:T(256)}, u32[]{:S(2)}) copy-start(f32[256]{0:T(256)} %param.27) | copy-start | bytes 3076
  61.3 30.0 %copy-start.6 = (f32[256]{0:T(256)S(1)}, f32[256]{0:T(256)}, u32[]{:S(2)}) copy-start(f32[256]{0:T(256)} %param.26) | copy-start | bytes 3076
Sparse Core Ops, SparseCore 0:
  9.5 42.9 all-gather.3
where the time goes:
time: 99.3 us; the launch traced here: 98.8 us
  blocking collectives  50.3 us (51%)
  between operations  15 us (15%)
  waiting for transfers between devices  10.9 us (11%)
  local copies, waits for them, and re-layouts  8.97 us (9%)
  matrix products  8.17 us (8%)
  other arithmetic  5.37 us (5%)
    all_gather x1, blocking collectives, per_device(): all_contexts = lax.all_gather(own_context, 'req', axis=0, tiled=True)  22.3 us
    all_gather x1, blocking collectives, per_device(): all_queries = lax.all_gather(queries, 'req', axis=0, tiled=True)  22.3 us
    all_gather x1, waiting for transfers between devices, per_device(): lax.all_gather(rel_table, 'req', axis=0, tiled=True)  10.1 us
    psum x1, blocking collectives, per_device(): row_sum = lax.psum(partial_out, 'tp')  5.75 us
    unnamed x22, local copies, waits for them, and re-layouts  3.5 us
    dot_general x2, matrix products, block_scores(): jnp.dot(one_back, rel_query, preferred_element_type=jnp.float32)  2.97 us
  transfers between devices with their start and end apart: 1, of which 1 were waited for; matrix products, arithmetic and copies ran while one was open for 11% of the time, Pallas kernels for 0%

commit v1 on v0

--- a/solution.py
+++ b/solution.py
@@ -10,6 +10,24 @@
 BLOCK = 512
 epsilon = 1e-06
 masked_score = -1e30
+
+
+def ring_gather(array, axis, dim):
+    ways, here, step = (lax.axis_size(axis), lax.axis_index(axis), array.shape[dim])
+    lengths = [n * ways if d == dim else n for d, n in enumerate(array.shape)]
+    full = lax.dynamic_update_slice_in_dim(
+        jnp.zeros(lengths, array.dtype), array, here * step, axis=dim
+    )
+    going_up = going_down = array
+    for far in range(1, ways // 2 + 1):
+        going_up = lax.ppermute(going_up, axis, [(d, (d + 1) % ways) for d in range(ways)])
+        full = lax.dynamic_update_slice_in_dim(full, going_up, (here - far) % ways * step, axis=dim)
+        if 2 * far < ways:
+            going_down = lax.ppermute(going_down, axis, [(d, (d - 1) % ways) for d in range(ways)])
+            full = lax.dynamic_update_slice_in_dim(
+                full, going_down, (here + far) % ways * step, axis=dim
+            )
+    return full
 
 
 def norm_rows(matrix):
@@ -115,7 +133,7 @@
             )
         )
     own_context = jnp.stack(contexts, axis=0)
-    all_contexts = lax.all_gather(own_context, "req", axis=0, tiled=True)
+    all_contexts = ring_gather(own_context, "req", 0)
     own_slots = lax.dynamic_slice_in_dim(slot_of, first_row, rows_dev, 0)
     picker = (own_slots[:, None] == jnp.arange(request_count, dtype=jnp.int32)[None, :]).astype(
         jnp.bfloat16

time: 99.3 us -> 103 us (1.037)
  blocking collectives: 50.3 us -> 28 us
  starting transfers between devices: 0.01 us -> 15.4 us
  waiting for transfers between devices: 10.9 us -> 21.5 us
    all_gather x1 -> x0, blocking collectives: 22.3 us -> none  [per_device(): all_contexts = lax.all_gather(own_context, 'req', axis=0, tiled=True)]
    ppermute x0 -> x7, starting transfers between devices: none -> 15.4 us  [the longest x4 7.72 us: ring_gather(): lax.ppermute(going_up, axis, [(d, (d + 1) % ways) for d in range(ways)])]
    ppermute x0 -> x7, waiting for transfers between devices: none -> 10 us  [the longest x4 10 us: ring_gather(): lax.ppermute(going_up, axis, [(d, (d + 1) % ways) for d in range(ways)])]
    unnamed x22 -> x23, local copies, waits for them, and re-layouts: 3.5 us -> 3.5 us
  transfers between devices with their start and end apart: 1 -> 8, of which waited for: 1 -> 5; matrix products, arithmetic and copies ran while one was open for 11% -> 10% of each run, Pallas kernels for 0% -> 0%
where the time goes in v1:
time: 103 us; the launch traced here: 102 us
  blocking collectives  28 us (27%)
  waiting for transfers between devices  21.5 us (21%)
  starting transfers between devices  15.4 us (15%)
  between operations  15.2 us (15%)
  local copies, waits for them, and re-layouts  8.39 us (8%)
  matrix products  8.16 us (8%)
  other arithmetic  5.38 us (5%)
    all_gather x1, blocking collectives, per_device(): all_queries = lax.all_gather(queries, 'req', axis=0, tiled=True)  22.3 us
    all_gather x1, waiting for transfers between devices, per_device(): lax.all_gather(rel_table, 'req', axis=0, tiled=True)  10.7 us
    ppermute x4, waiting for transfers between devices, ring_gather(): lax.ppermute(going_up, axis, [(d, (d + 1) % ways) for d in range(ways)])  10 us
    ppermute x4, starting transfers between devices, ring_gather(): lax.ppermute(going_up, axis, [(d, (d + 1) % ways) for d in range(ways)])  7.72 us
    ppermute x3, starting transfers between devices, ring_gather(): lax.ppermute(going_down, axis, [(d, (d - 1) % ways) for d in range(ways)])  7.66 us
    psum x1, blocking collectives, per_device(): row_sum = lax.psum(partial_out, 'tp')  5.75 us
    unnamed x23, local copies, waits for them, and re-layouts  3.5 us
    dot_general x2, matrix products, block_scores(): jnp.dot(one_back, rel_query, preferred_element_type=jnp.float32)  2.96 us
  transfers between devices with their start and end apart: 8, of which 5 were waited for; matrix products, arithmetic and copies ran while one was open for 10% of the time, Pallas kernels for 0%

profile of v1, /device:TPU:0, one launch (start us, length us, event | category | flops | bytes accessed | tf_op | source)
XLA Modules:
  0.0 102.1 jit_solution(6528186047661797971)
XLA Ops:
  6.5 0.7 all-gather.3.cloned.1.call-update
  7.4 1.4 %fusion.54 = (s32[1]{0:T(128)}, s32[1]{0:T(128)}) fusion(s32[2]{0:T(128)} %param.20), kind=kLoop, calls=%fused_computation.98 | loop fusion | bytes 16 | tf_op jit(solution)/shard_map/slice | solution.py:130
  10.2 0.9 fusion.25
  11.1 22.3 %all-gather = bf16[8,2,256]{2,1,0:T(2,128)(2,1)S(1)} all-gather(bf16[1,2,256]{2,1,0:T(2,128)(2,1)S(1)} %fusion.25), channel_id=1, replica_groups=mesh['req'=8,'tp'=4] {'req'}, dimensions={0}, use_global_device_ids=true | all-gather | bytes 9216 | tf_op jit(solution)/shard_map/all_gather | solution.py:114
  33.3 0.8 convolution_convert_fusion.4
  34.4 1.5 %fusion.52 = (bf16[1,1536,256]{2,1,0:T(8,128)(2,1)S(1)}, bf16[1,1536,256]{2,1,0:T(8,128)(2,1)S(1)}) fusion(bf16[2,1536,256]{2,1,0:T(8,128)(2,1)} %param.18), kind=kLoop, calls=%fused_computation.96 | loop fusion | bytes 3145728 | tf_op jit(solution)/shard_map/slice | solution.py:127
  35.8 1.2 %copy.33 = bf16[1,1536,256]{1,2,0:T(8,128)(2,1)} copy(bf16[1,1536,256]{2,1,0:T(8,128)(2,1)S(1)} %get-tuple-element.141) | data formatting | bytes 1572864
  37.0 1.2 %copy.35 = bf16[1,1536,256]{1,2,0:T(8,128)(2,1)} copy(bf16[1,1536,256]{2,1,0:T(8,128)(2,1)S(1)} %get-tuple-element.142) | data formatting | bytes 1572864
  38.2 1.5 %fusion.53 = (bf16[1,1536,256]{2,1,0:T(8,128)(2,1)S(1)}, bf16[1,1536,256]{2,1,0:T(8,128)(2,1)S(1)}) fusion(bf16[2,1536,256]{2,1,0:T(8,128)(2,1)} %param.19), kind=kLoop, calls=%fused_computation.97 | loop fusion | bytes 3145728 | tf_op jit(solution)/shard_map/slice | solution.py:128
  39.7 0.3 copy.34
  40.0 0.3 copy.36
  40.3 0.7 iota_compare_fusion.9
  41.0 0.7 iota_compare_fusion.8
  41.7 10.7 %all-gather.3.cloned.1.call-done = bf16[512,1024]{1,0:T(8,128)(2,1)} async-done(((bf16[64,1024]{1,0:T(8,128)(2,1)}), bf16[512,1024]{1,0:T(8,128)(2,1)}) %all-gather.3.cloned.1.call-update) | async-done | bytes 1048592 | tf_op jit(solution)/shard_map/all_gather | solution.py:110
  52.5 1.5 %convert_reduce_fusion = f32[512]{0:T(512)S(1)} fusion(bf16[512,1024]{1,0:T(8,128)(2,1)} %all-gather.3.cloned.1.call-done), kind=kLoop, calls=%fused_computation.35 | loop fusion | flops 1048064 | bytes 1050624 | tf_op jit(solution)/shard_map/reduce_sum | solution.py:34
  54.0 0.4 fusion.22
  54.4 0.5 convolution_convert_fusion
  54.9 0.5 copy-done.7
  55.5 0.5 convolution_convert_fusion.1
  56.0 2.4 %while.20 = (s32[]{:T(128)}, f32[4,1536]{1,0:T(4,128)S(1)}, s32[]{:T(128)}, bf16[1536,256]{0,1:T(8,128)(2,1)}, bf16[4,64]{1,0:T(4,128)(2,1)S(1)}, /*index=5*/s32...) while((s32[]{:T(128)}, f32[4,1536]{1,0:T(4,128)S(1)}, ...), condition=%wide.region_4.5_spmd, body=%wide.region_2.4_spmd.sunk | while | flops 269882368 | bytes 1903791 | solution.py:80
  56.1 0.5 fusion.98
  56.6 0.1 fusion.99
  56.7 1.5 %multiply_reduce_fusion.5 = (f32[512,4]{0,1:T(4,128)S(1)}, bf16[512,256]{0,1:T(8,128)(2,1)S(1)}) fusion(bf16[1536,256]{0,1:T(8,128)(2,1)} %get-tuple-element.326, s32[]{:T(128)S(6)} %select_n.143, bf16[512,256]{1,0:T(8,128)(2,1)S(1)} %get-tuple-element.330, s32[512]{0:T(512)S(1)} %get-tuple-element.247), kind=kOutput, calls=%fused_computation.4.clone.1 | convolution fusion | flops 134871040 | bytes 796676 | tf_op jit(solution)/shard_map/while/body/dot_general | solution.py:60
  58.2 0.1 fusion.100
  58.4 0.1 select_reduce_fusion.1
  58.5 0.2 fusion.30
  58.8 2.4 %while.21 = (s32[]{:T(128)}, f32[4,1536]{1,0:T(4,128)S(1)}, s32[]{:T(128)}, bf16[1536,256]{0,1:T(8,128)(2,1)}, bf16[4,64]{1,0:T(4,128)(2,1)S(1)}, /*index=5*/s32...) while((s32[]{:T(128)}, f32[4,1536]{1,0:T(4,128)S(1)}, ...), condition=%wide.region_9.10_spmd, body=%wide.region_7.9_spmd.sunk | while | flops 269882368 | bytes 1903791 | solution.py:80
  58.9 0.5 fusion.108
  59.4 0.1 fusion.109
  59.6 1.5 %multiply_reduce_fusion.6 = (f32[512,4]{0,1:T(4,128)S(1)}, bf16[512,256]{0,1:T(8,128)(2,1)S(1)}) fusion(bf16[1536,256]{0,1:T(8,128)(2,1)} %get-tuple-element.290, s32[]{:T(128)S(6)} %select_n.144, bf16[512,256]{1,0:T(8,128)(2,1)S(1)} %get-tuple-element.294, s32[512]{0:T(512)S(1)} %get-tuple-element.259), kind=kOutput, calls=%fused_computation.21.clone.1 | convolution fusion | flops 134871040 | bytes 796676 | tf_op jit(solution)/shard_map/while/body/dot_general | solution.py:60
  61.1 0.1 fusion.110
  61.3 0.1 select_reduce_fusion
  61.4 0.2 fusion.31
  61.7 0.3 fusion.28
  62.1 0.3 fusion.26
  62.6 5.4 %collective-permute-start = (bf16[2,256]{1,0:T(2,128)(2,1)S(1)}, bf16[2,256]{1,0:T(2,128)(2,1)S(1)}, u32[]{:S(2)}, u32[]{:S(2)}) collective-permute-start(bf16[2,256]{1,0:T(2,128)(2,1)S(1)} %get-tuple-element.140), channel_id=1, source_target_pairs={{0,4},{4,8},{8,12},{12,16},{16,20},{20,24},{24,28},{28,0},{1,5},{5... | collective-permute-start | bytes 3080 | tf_op jit(solution)/shard_map/ppermute | solution.py:23
  68.1 1.2 %collective-permute-done = bf16[2,256]{1,0:T(2,128)(2,1)S(1)} collective-permute-done((bf16[2,256]{1,0:T(2,128)(2,1)S(1)}, bf16[2,256]{1,0:T(2,128)(2,1)S(1)}, u32[]{:S(2)}, u32[]{:S(2)}) %collective-permute-start) | collective-permute-done | bytes 1056 | tf_op jit(solution)/shard_map/ppermute | solution.py:23
  69.3 2.3 %collective-permute-start.2 = (bf16[2,256]{1,0:T(2,128)(2,1)S(1)}, bf16[2,256]{1,0:T(2,128)(2,1)S(1)}, u32[]{:S(2)}, u32[]{:S(2)}) collective-permute-start(bf16[2,256]{1,0:T(2,128)(2,1)S(1)} %collective-permute-done), channel_id=1, source_target_pairs={{0,4},{4,8},{8,12},{12,16},{16,20},{20,24},{24,28},{28,0},{1,5},{5... | collective-permute-start | bytes 3080 | tf_op jit(solution)/shard_map/ppermute | solution.py:23
  71.6 2.7 %collective-permute-start.3 = (bf16[2,256]{1,0:T(2,128)(2,1)S(1)}, bf16[2,256]{1,0:T(2,128)(2,1)S(1)}, u32[]{:S(2)}, u32[]{:S(2)}) collective-permute-start(bf16[2,256]{1,0:T(2,128)(2,1)S(1)} %collective-permute-done.1), channel_id=1, source_target_pairs={{0,28},{4,0},{8,4},{12,8},{16,12},{20,16},{24,20},{28,24},{1,29},{... | collective-permute-start | bytes 3080 | tf_op jit(solution)/shard_map/ppermute | solution.py:26
  74.3 1.3 %collective-permute-done.2 = bf16[2,256]{1,0:T(2,128)(2,1)S(1)} collective-permute-done((bf16[2,256]{1,0:T(2,128)(2,1)S(1)}, bf16[2,256]{1,0:T(2,128)(2,1)S(1)}, u32[]{:S(2)}, u32[]{:S(2)}) %collective-permute-start.2) | collective-permute-done | bytes 1056 | tf_op jit(solution)/shard_map/ppermute | solution.py:23
  75.6 5.0 %collective-permute-start.5 = (bf16[2,256]{1,0:T(2,128)(2,1)S(1)}, bf16[2,256]{1,0:T(2,128)(2,1)S(1)}, u32[]{:S(2)}, u32[]{:S(2)}) collective-permute-start(bf16[2,256]{1,0:T(2,128)(2,1)S(1)} %collective-permute-done.3), channel_id=1, source_target_pairs={{0,28},{4,0},{8,4},{12,8},{16,12},{20,16},{24,20},{28,24},{1,29},{... | collective-permute-start | bytes 3080 | tf_op jit(solution)/shard_map/ppermute | solution.py:26
  80.6 1.3 %collective-permute-done.4 = bf16[2,256]{1,0:T(2,128)(2,1)S(1)} collective-permute-done((bf16[2,256]{1,0:T(2,128)(2,1)S(1)}, bf16[2,256]{1,0:T(2,128)(2,1)S(1)}, u32[]{:S(2)}, u32[]{:S(2)}) %collective-permute-start.4) | collective-permute-done | bytes 1056 | tf_op jit(solution)/shard_map/ppermute | solution.py:23
  81.9 6.2 %collective-permute-done.6 = bf16[2,256]{1,0:T(2,128)(2,1)S(1)} collective-permute-done((bf16[2,256]{1,0:T(2,128)(2,1)S(1)}, bf16[2,256]{1,0:T(2,128)(2,1)S(1)}, u32[]{:S(2)}, u32[]{:S(2)}) %collective-permute-start.6) | collective-permute-done | bytes 1056 | tf_op jit(solution)/shard_map/ppermute | solution.py:23
  88.1 0.3 fusion.24
  88.4 5.7 %psum.7 = f32[2,1024]{1,0:T(2,128)S(1)} all-reduce(f32[2,1024]{1,0:T(2,128)S(1)} %fusion.24), channel_id=1, replica_groups=mesh['req'=8,'tp'=4] {'tp'}, use_global_device_ids=true, to_apply=%region_12.13 | all-reduce | flops 2048 | bytes 16384 | tf_op jit(solution)/shard_map/psum | solution.py:146
  94.2 0.1 fusion.35
  94.3 0.2 multiply_reduce_fusion.2
  94.6 0.6 fusion.39
  (56 shorter events, 1.1 us)
Async XLA Ops:
  6.5 3.6 %copy-start = (bf16[1024,256]{1,0:T(8,128)(2,1)S(1)}, bf16[1024,256]{1,0:T(8,128)(2,1)}, u32[]{:S(2)}) copy-start(bf16[1024,256]{1,0:T(8,128)(2,1)} %param.23) | copy-start | bytes 1572868
  6.5 45.9 %all-gather.3.cloned.1.call-start = ((), (), s32[]{:S(2)}) async-start(), calls=%async_computation | async-start | bytes 1179648 | tf_op jit(solution)/shard_map/all_gather | solution.py:110
  39.7 2.0 %copy-start.4 = (s32[2,1536]{1,0:T(2,128)S(1)}, s32[2,1536]{1,0:T(2,128)}, u32[]{:S(2)}) copy-start(s32[2,1536]{1,0:T(2,128)} %param.21) | copy-start | bytes 36868
  52.5 1.5 %copy-start.1 = (bf16[512,1024]{1,0:T(8,128)(2,1)S(1)}, bf16[512,1024]{1,0:T(8,128)(2,1)}, u32[]{:S(2)}) copy-start(bf16[512,1024]{1,0:T(8,128)(2,1)} %all-gather.3.cloned.1.call-done) | copy-start | bytes 3145732
  54.4 1.0 %copy-start.7 = (bf16[1024,256]{1,0:T(8,128)(2,1)S(1)}, bf16[1024,256]{1,0:T(8,128)(2,1)}, u32[]{:S(2)}) copy-start(bf16[1024,256]{1,0:T(8,128)(2,1)} %param.24) | copy-start | bytes 1572868
  61.2 6.8 %copy-start.8 = (s32[16]{0:T(128)S(1)}, s32[16]{0:T(128)}, u32[]{:S(2)}) copy-start(s32[16]{0:T(128)} %param.17) | copy-start | bytes 196
  61.2 26.9 %copy-start.2 = (bf16[256,1024]{1,0:T(8,128)(2,1)S(1)}, bf16[256,1024]{1,0:T(8,128)(2,1)}, u32[]{:S(2)}) copy-start(bf16[256,1024]{1,0:T(8,128)(2,1)} %param.25) | copy-start | bytes 1572868
  61.3 32.9 %copy-start.3 = (bf16[2,1024]{1,0:T(2,128)(2,1)S(1)}, bf16[2,1024]{1,0:T(2,128)(2,1)}, u32[]{:S(2)}) copy-start(bf16[2,1024]{1,0:T(2,128)(2,1)} %param.16) | copy-start | bytes 12292
  61.3 33.3 %copy-start.5 = (f32[256]{0:T(256)S(1)}, f32[256]{0:T(256)}, u32[]{:S(2)}) copy-start(f32[256]{0:T(256)} %param.27) | copy-start | bytes 3076
  61.3 33.3 %copy-start.6 = (f32[256]{0:T(256)S(1)}, f32[256]{0:T(256)}, u32[]{:S(2)}) copy-start(f32[256]{0:T(256)} %param.26) | copy-start | bytes 3076
  62.6 6.7 %collective-permute-start = (bf16[2,256]{1,0:T(2,128)(2,1)S(1)}, bf16[2,256]{1,0:T(2,128)(2,1)S(1)}, u32[]{:S(2)}, u32[]{:S(2)}) collective-permute-start(bf16[2,256]{1,0:T(2,128)(2,1)S(1)} %get-tuple-element.140), channel_id=1, source_target_pairs={{0,4},{4,8},{8,12},{12,16},{16,20},{20,24},{24,28},{28,0},{1,5},{5... | collective-permute-start | bytes 3080 | tf_op jit(solution)/shard_map/ppermute | solution.py:23
  68.0 3.6 %collective-permute-start.1 = (bf16[2,256]{1,0:T(2,128)(2,1)S(1)}, bf16[2,256]{1,0:T(2,128)(2,1)S(1)}, u32[]{:S(2)}, u32[]{:S(2)}) collective-permute-start(bf16[2,256]{1,0:T(2,128)(2,1)S(1)} %get-tuple-element.140), channel_id=1, source_target_pairs={{0,28},{4,0},{8,4},{12,8},{16,12},{20,16},{24,20},{28,24},{1,29},{... | collective-permute-start | bytes 3080 | tf_op jit(solution)/shard_map/ppermute | solution.py:26
  69.3 6.3 %collective-permute-start.2 = (bf16[2,256]{1,0:T(2,128)(2,1)S(1)}, bf16[2,256]{1,0:T(2,128)(2,1)S(1)}, u32[]{:S(2)}, u32[]{:S(2)}) collective-permute-start(bf16[2,256]{1,0:T(2,128)(2,1)S(1)} %collective-permute-done), channel_id=1, source_target_pairs={{0,4},{4,8},{8,12},{12,16},{16,20},{20,24},{24,28},{28,0},{1,5},{5... | collective-permute-start | bytes 3080 | tf_op jit(solution)/shard_map/ppermute | solution.py:23
  71.6 4.0 %collective-permute-start.3 = (bf16[2,256]{1,0:T(2,128)(2,1)S(1)}, bf16[2,256]{1,0:T(2,128)(2,1)S(1)}, u32[]{:S(2)}, u32[]{:S(2)}) collective-permute-start(bf16[2,256]{1,0:T(2,128)(2,1)S(1)} %collective-permute-done.1), channel_id=1, source_target_pairs={{0,28},{4,0},{8,4},{12,8},{16,12},{20,16},{24,20},{28,24},{1,29},{... | collective-permute-start | bytes 3080 | tf_op jit(solution)/shard_map/ppermute | solution.py:26
  75.6 6.3 %collective-permute-start.4 = (bf16[2,256]{1,0:T(2,128)(2,1)S(1)}, bf16[2,256]{1,0:T(2,128)(2,1)S(1)}, u32[]{:S(2)}, u32[]{:S(2)}) collective-permute-start(bf16[2,256]{1,0:T(2,128)(2,1)S(1)} %collective-permute-done.2), channel_id=1, source_target_pairs={{0,4},{4,8},{8,12},{12,16},{16,20},{20,24},{24,28},{28,0},{1,5},{5... | collective-permute-start | bytes 3080 | tf_op jit(solution)/shard_map/ppermute | solution.py:23
  75.6 6.3 %collective-permute-start.5 = (bf16[2,256]{1,0:T(2,128)(2,1)S(1)}, bf16[2,256]{1,0:T(2,128)(2,1)S(1)}, u32[]{:S(2)}, u32[]{:S(2)}) collective-permute-start(bf16[2,256]{1,0:T(2,128)(2,1)S(1)} %collective-permute-done.3), channel_id=1, source_target_pairs={{0,28},{4,0},{8,4},{12,8},{16,12},{20,16},{24,20},{28,24},{1,29},{... | collective-permute-start | bytes 3080 | tf_op jit(solution)/shard_map/ppermute | solution.py:26
  81.8 6.3 %collective-permute-start.6 = (bf16[2,256]{1,0:T(2,128)(2,1)S(1)}, bf16[2,256]{1,0:T(2,128)(2,1)S(1)}, u32[]{:S(2)}, u32[]{:S(2)}) collective-permute-start(bf16[2,256]{1,0:T(2,128)(2,1)S(1)} %collective-permute-done.4), channel_id=1, source_target_pairs={{0,4},{4,8},{8,12},{12,16},{16,20},{20,24},{24,28},{28,0},{1,5},{5... | collective-permute-start | bytes 3080 | tf_op jit(solution)/shard_map/ppermute | solution.py:23
Sparse Core Ops, SparseCore 0:
  9.5 42.9 all-gather.2
